TPU v7x, 256 devices: a whole 4x4x8 slice. The times are simulated.
256 devices in a mesh: energy: 4 (over z_lo), cluster: 16 (over x, y), tile: 4 (over z_hi, core).
Axes of the slice: x: 4, y: 4, z: 8 (z_hi: 2, z_lo: 4; z = z_hi * 4 + z_lo), core: 2. Of those that a mesh axis runs over, the one named last changes fastest.
Arguments:
- boundary: bfloat16 [16, 2, 512, 8, 2, 1024], P('cluster', None, 'tile', 'energy'), may hold values from -5 to 5
- column_source: int32 [16, 1024], P('cluster'), may hold values from 0 to 1023, as said below
- energy_weights: float32 [8], P('energy'), may hold values from 0.2 to 2
Outputs:
- final_rows: float32 [16, 256, 8, 2, 1024], P('cluster', 'tile', 'energy')
- density: float32 [16, 256], P('cluster', 'tile')
Inputs may be any that keep to these rules, and one draw needn't show every extreme that they name: `column_source`: for each cluster, every index 0 to 1023 appears once.
All inputs are finite; a program needn't handle non-finite values.
Results may differ from a plain program's by a relative error of at most 0.015.
Values may be sent and summed in bfloat16 or wider, within the bound.
No kernel may reach another device: no remote copies, remote signals or barrier semaphores. Data moves between devices by JAX's collectives and lax.ppermute only.
A program may use at most 64 MiB of HBM per device.

v0:
```python
import jax
import jax.numpy as jnp
from jax import lax
from jax.sharding import PartitionSpec as P


def swapped(shard, axis, distance):
    return lax.ppermute(shard, axis, [(i, i ^ 1 << distance) for i in range(lax.axis_size(axis))])


def complex_product(left, right):

    def single(first_part, second_part):
        return jnp.einsum(
            "mek,ken->men", first_part, second_part, preferred_element_type=jnp.float32
        )

    real_part = single(left[:, :, 0], right[:, :, 0]) - single(left[:, :, 1], right[:, :, 1])
    imag_part = single(left[:, :, 0], right[:, :, 1]) + single(left[:, :, 1], right[:, :, 0])
    return jnp.stack([real_part, imag_part], axis=2)


def inverse_guess(interior):
    values = interior.astype(jnp.float32)
    diagonal = jnp.diagonal(values, axis1=0, axis2=3)
    denom = diagonal[:, 0] * diagonal[:, 0] + diagonal[:, 1] * diagonal[:, 1]
    inv_real = diagonal[:, 0] / denom
    inv_imag = -diagonal[:, 1] / denom
    column_real = inv_real[None, :, :]
    column_imag = inv_imag[None, :, :]
    row_real = inv_real.T[:, :, None]
    row_imag = inv_imag.T[:, :, None]
    values_real = values[:, :, 0]
    values_imag = values[:, :, 1]
    temp_real = values_real * column_real - values_imag * column_imag
    temp_imag = values_real * column_imag + values_imag * column_real
    prod_real = row_real * temp_real - row_imag * temp_imag
    prod_imag = row_real * temp_imag + row_imag * temp_real
    ident = jnp.eye(values.shape[0], dtype=jnp.float32)[:, None, :]
    guess_real = 2.0 * ident * row_real - prod_real
    guess_imag = 2.0 * ident * row_imag - prod_imag
    return jnp.stack([guess_real, guess_imag], axis=2).astype(jnp.bfloat16)


def place_block(block, is_low):
    zeros = jnp.zeros_like(block)
    return jnp.where(
        is_low, jnp.concatenate([block, zeros], axis=3), jnp.concatenate([zeros, block], axis=3)
    )


def swap_separator(separator, level_index):
    return swapped(separator, "cluster", level_index)


def eliminate(outer_coupling, start_block, interior, approx_inverse, coupling_rows):
    applied = complex_product(outer_coupling.astype(jnp.bfloat16), approx_inverse)
    middle = complex_product(applied.astype(jnp.bfloat16), interior).astype(jnp.bfloat16)
    reduced = (2.0 * applied - complex_product(middle, approx_inverse)).astype(jnp.bfloat16)
    row_piece = lax.all_gather(coupling_rows, "tile", axis=0, tiled=True)
    columns = lax.slice_in_dim(reduced, 0, row_piece.shape[0], axis=3)
    return start_block - complex_product(columns, row_piece)


def per_device(boundary, column_source, energy_weights):
    stored = boundary[0]
    canonical = jnp.take(stored, column_source[0], axis=4)
    separator = canonical[0]
    outer_rows = canonical[1]
    interior_width = separator.shape[3] // 2
    row_count = separator.shape[0]
    levels = min(2, lax.axis_size("cluster") // 2)
    cluster_index = lax.axis_index("cluster")
    tile_index = lax.axis_index("tile")
    for level_index in range(levels):
        side_bit = cluster_index // 2**level_index % 2
        is_low = side_bit == 0
        final_level = level_index == levels - 1
        if final_level:
            partner_outer = outer_rows
            partner_sep = swap_separator(separator, level_index)
        else:
            partner_sep, partner_outer = swapped((separator, outer_rows), "cluster", level_index)
            separator = separator.astype(jnp.float32)
            outer_rows = outer_rows.astype(jnp.float32)
            partner_sep = partner_sep.astype(jnp.float32)
            partner_outer = partner_outer.astype(jnp.float32)
        interior_rows = (
            separator[..., :interior_width] + partner_sep[..., :interior_width]
        ).astype(jnp.bfloat16)
        interior = lax.all_gather(interior_rows, "tile", axis=0, tiled=True)
        approx_inverse = inverse_guess(interior)
        low_sep = jnp.where(is_low, separator, partner_sep)
        high_sep = jnp.where(is_low, partner_sep, separator)
        coupling_rows = jnp.concatenate(
            [low_sep[..., interior_width:], high_sep[..., interior_width:]], axis=3
        ).astype(jnp.bfloat16)
        if final_level:
            share = row_count // 2**level_index
            within = cluster_index % 2**level_index
            own_rows = lax.dynamic_slice_in_dim(outer_rows, within * share, share, 0)
            new_rows = eliminate(
                own_rows[..., :interior_width],
                place_block(own_rows[..., interior_width:], is_low),
                interior,
                approx_inverse,
                coupling_rows,
            )
            columns = (
                side_bit * interior_width
                + tile_index * row_count
                + within * share
                + jnp.arange(share, dtype=jnp.int32)
            )
            selector = (
                jnp.arange(new_rows.shape[3], dtype=jnp.int32)[None, :] == columns[:, None]
            ).astype(jnp.float32)
            diagonal = jnp.sum(new_rows[:, :, 1, :] * selector[:, None, :], axis=2)
            partial_sum = jnp.sum(diagonal * energy_weights[None, :], axis=1)
            density = lax.psum(partial_sum, "energy")
            return (new_rows[None], density[None])
        else:
            low_outer = jnp.where(is_low, outer_rows, partner_outer)
            high_outer = jnp.where(is_low, partner_outer, outer_rows)
            outer_coupling = jnp.concatenate(
                [low_outer[..., :interior_width], high_outer[..., :interior_width]], axis=0
            )
            start_block = jnp.concatenate(
                [
                    place_block(low_outer[..., interior_width:], True),
                    place_block(high_outer[..., interior_width:], False),
                ],
                axis=0,
            )
            merged = eliminate(outer_coupling, start_block, interior, approx_inverse, coupling_rows)
            separator = merged[:row_count]
            outer_rows = merged[row_count:]


def solution(mesh):
    placed = (P("cluster", None, "tile", "energy", None, None), P("cluster", None), P("energy"))
    return jax.shard_map(
        per_device,
        mesh=mesh,
        in_specs=placed,
        out_specs=(P("cluster", "tile", "energy", None, None), P("cluster", "tile")),
        check_vma=False,
    )
```

profile of v0, /device:TPU:2, one launch (start us, length us, event | category | flops | bytes accessed | tf_op | source)
XLA Modules:
  0.0 364.8 jit_solution(14689596253726604121)
XLA Ops:
  7.2 8.9 %copy.65 = bf16[1,2,128,2,2,1024]{2,4,5,3,1,0:T(2,128)(2,1)S(1)} copy(bf16[1,2,128,2,2,1024]{5,4,3,2,1,0:T(2,128)(2,1)} %param.3) | data formatting | bytes 4194304 | tf_op args[0]
  16.2 12.1 %gather_fusion = bf16[1024,2,128,2,2]{2,4,3,1,0:T(2,128)(2,1)} fusion(bf16[2,128,2,2,1024]{1,3,4,2,0:T(2,128)(2,1)S(1)} %bitcast.255, s32[1024]{0:T(1024)S(1)} %broadcast_clamp_fusion), kind=kCustom, calls=%fused_computation | custom fusion | bytes 4198400 | tf_op jit(solution)/shard_map/jit(_take)/gather | solution.py:67
  28.3 6.1 %copy.66 = bf16[1024,2,128,2,2]{0,2,3,4,1:T(8,128)(2,1)} copy(bf16[1024,2,128,2,2]{2,4,3,1,0:T(2,128)(2,1)} %gather_fusion) | data formatting | bytes 4194304 | tf_op jit(solution)/shard_map/jit(_take)/gather | solution.py:67
  34.5 1.8 select_bitcast_fusion
  36.3 1.4 fusion.58
  37.7 1.6 collective-permute-start.1
  39.2 23.3 %collective-permute-done.1 = bf16[128,2,2,1024]{3,0,1,2:T(8,128)(2,1)S(1)} collective-permute-done((bf16[128,2,2,1024]{3,0,1,2:T(8,128)(2,1)S(1)}, bf16[128,2,2,1024]{3,0,1,2:T(8,128)(2,1)S(1)}, u32[]{:S(2)}, u32[]{:S(2)}) %collective-permute-start.1) | collective-permute-done | bytes 1048608 | tf_op jit(solution)/shard_map/ppermute | solution.py:8
  62.8 1.3 copy-done.5
  64.2 1.0 fusion.36
  65.2 1.7 collective-permute-start
  66.9 1.7 select_convert_fusion.3
  68.5 1.1 pad_maximum_fusion.1
  69.9 19.8 %collective-permute-done = bf16[128,2,2,1024]{3,0,1,2:T(8,128)(2,1)} collective-permute-done((bf16[128,2,2,1024]{3,0,1,2:T(8,128)(2,1)}, bf16[128,2,2,1024]{3,0,1,2:T(8,128)(2,1)}, u32[]{:S(2)}, u32[]{:S(2)}) %collective-permute-start) | collective-permute-done | bytes 1048608 | tf_op jit(solution)/shard_map/ppermute | solution.py:8
  89.6 1.8 convert_select_fusion.1
  91.6 1.0 slice.266
  92.7 1.0 slice.267
  93.7 17.7 %all-gather.7.cloned.1.call-done = bf16[512,2,2,512]{3,0,1,2:T(8,128)(2,1)} async-done(((bf16[128,2,2,512]{3,0,1,2:T(8,128)(2,1)}), bf16[512,2,2,512]{3,0,1,2:T(8,128)(2,1)}) %all-gather.7.cloned.1.call-update) | async-done | bytes 2097168 | tf_op jit(solution)/shard_map/all_gather | solution.py:91
  111.5 4.3 %fusion.65 = (f32[512,2,2,512]{3,0,1,2:T(8,128)}, f32[2,2,512,512]{3,2,0,1:T(8,128)S(1)}) fusion(bf16[512,2,2,512]{3,0,1,2:T(8,128)(2,1)} %all-gather.7.cloned.1.call-done), kind=kLoop, calls=%fused_computation.154 | loop fusion | flops 1048576 | bytes 10485760 | tf_op jit(solution)/shard_map/convert_element_type | solution.py:24
  115.7 5.2 %copy.67 = f32[2,2,512,512]{3,1,2,0:T(2,128)} copy(f32[2,2,512,512]{3,2,0,1:T(8,128)S(1)} %get-tuple-element.23) | data formatting | bytes 8388608 | tf_op jit(solution)/shard_map/jit(diagonal)/transpose | solution.py:25
  121.0 7.5 %gather_fusion.1 = f32[512,2,2]{0,2,1:T(2,128)S(1)} fusion(f32[2,2,512,512]{3,1,2,0:T(2,128)} %copy.67, s32[512]{0:T(512)S(1)} %bitcast.253), kind=kCustom, calls=%fused_computation.1 | custom fusion | bytes 20480 | tf_op jit(solution)/shard_map/jit(diagonal)/gather | solution.py:25
  128.5 2.9 fusion.31
  131.4 0.5 fusion.61
  131.9 0.5 fusion.14
  132.4 0.5 fusion.59
  133.0 0.5 fusion.13
  133.7 1.4 copy-done
  135.1 0.5 fusion.38
  135.7 0.5 fusion.18
  136.2 0.5 fusion.68
  136.7 0.5 fusion.39
  137.3 0.5 fusion.17
  137.8 0.5 fusion.12
  138.4 0.5 fusion.69
  138.9 0.5 fusion.11
  139.9 36.3 %all-gather.5.cloned.1.call-done = bf16[512,2,2,1024]{3,0,1,2:T(8,128)(2,1)} async-done(((bf16[128,2,2,1024]{3,0,1,2:T(8,128)(2,1)}), bf16[512,2,2,1024]{3,0,1,2:T(8,128)(2,1)}) %all-gather.5.cloned.1.call-update) | async-done | bytes 4194320 | tf_op jit(solution)/shard_map/all_gather | solution.py:60
  176.1 2.5 fusion.3
  178.9 0.8 fusion.2
  179.7 0.8 subtract_bitcast_fusion
  180.5 0.8 add_bitcast_fusion
  181.3 0.4 copy-done.7
  182.1 0.8 fusion
  182.9 0.6 fusion.63
  183.5 1.3 copy-done.9
  184.8 3.0 collective-permute-start.2
  187.9 46.3 %collective-permute-done.2 = f32[128,2,2,1024]{3,0,1,2:T(8,128)S(1)} collective-permute-done((f32[128,2,2,1024]{3,0,1,2:T(8,128)S(1)}, f32[128,2,2,1024]{3,0,1,2:T(8,128)S(1)}, u32[]{:S(2)}, u32[]{:S(2)}) %collective-permute-start.2) | collective-permute-done | bytes 2097184 | tf_op jit(solution)/shard_map/ppermute | solution.py:8
  234.1 1.3 copy-done.11
  235.4 1.0 fusion.35
  236.5 1.7 select_convert_fusion.1
  238.2 1.1 pad_maximum_fusion.2
  239.4 0.9 dynamic-slice_convert_fusion
  240.3 1.1 constant_dynamic-slice_fusion
  241.4 34.5 %all-gather.11.cloned.1.call-done = bf16[512,2,2,512]{3,0,1,2:T(8,128)(2,1)} async-done(((bf16[128,2,2,512]{3,0,1,2:T(8,128)(2,1)}), bf16[512,2,2,512]{3,0,1,2:T(8,128)(2,1)}) %all-gather.11.cloned.1.call-update) | async-done | bytes 2097168 | tf_op jit(solution)/shard_map/all_gather | solution.py:91
  275.9 4.3 %fusion.64 = (f32[512,2,2,512]{3,0,1,2:T(8,128)}, f32[2,2,512,512]{3,2,0,1:T(8,128)S(1)}) fusion(bf16[512,2,2,512]{3,0,1,2:T(8,128)(2,1)} %all-gather.11.cloned.1.call-done), kind=kLoop, calls=%fused_computation.153 | loop fusion | flops 1048576 | bytes 10485760 | tf_op jit(solution)/shard_map/convert_element_type | solution.py:24
  280.2 5.2 %copy.95 = f32[2,2,512,512]{3,1,2,0:T(2,128)} copy(f32[2,2,512,512]{3,2,0,1:T(8,128)S(1)} %get-tuple-element.21) | data formatting | bytes 8388608 | tf_op jit(solution)/shard_map/jit(diagonal)/transpose | solution.py:25
  285.4 7.2 %gather_fusion.2 = f32[512,2,2]{0,2,1:T(2,128)S(1)} fusion(f32[2,2,512,512]{3,1,2,0:T(2,128)} %copy.95, s32[512]{0:T(512)S(1)} %bitcast.254), kind=kCustom, calls=%fused_computation.2 | custom fusion | bytes 20480 | tf_op jit(solution)/shard_map/jit(diagonal)/gather | solution.py:25
  292.7 2.9 fusion.33
  296.8 0.9 copy-done.1
  300.3 40.8 %all-gather.9.cloned.1.call-done = bf16[512,2,2,1024]{3,0,1,2:T(8,128)(2,1)} async-done(((bf16[128,2,2,1024]{3,0,1,2:T(8,128)(2,1)}), bf16[512,2,2,1024]{3,0,1,2:T(8,128)(2,1)}) %all-gather.9.cloned.1.call-update) | async-done | bytes 4194320 | tf_op jit(solution)/shard_map/all_gather | solution.py:60
  341.0 2.2 fusion.6
  343.3 2.1 fusion.7
  345.4 0.5 fusion.22
  345.8 0.5 fusion.20
  347.2 9.2 %psum.7 = f32[1,64]{1,0:T(1,128)} all-reduce(f32[1,64]{1,0:T(1,128)S(1)} %bitcast.264), channel_id=1, replica_groups=mesh['energy'=4,'cluster'=16,'tile'=4] {'energy'}, use_global_device_ids=true, to_apply=%region_2.3 | all-reduce | flops 64 | bytes 512 | tf_op jit(solution)/shard_map/psum | solution.py:120
  356.5 1.8 copy.99
  (64 shorter events, 6.7 us)
Async XLA Ops:
  7.2 9.0 %copy-start.12 = (s32[1,1024]{1,0:T(1,128)S(1)}, s32[1,1024]{1,0:T(1,128)}, u32[]{:S(2)}) copy-start(s32[1,1024]{1,0:T(1,128)} %param.4) | copy-start | bytes 12292
  7.2 104.3 %all-gather.7.cloned.1.call-start = ((), (), s32[]{:S(2)}) async-start(), calls=%async_computation.1 | async-start | bytes 2621440 | tf_op jit(solution)/shard_map/all_gather | solution.py:91
  37.7 25.2 %copy-start.4 = (f32[128,2,2,1024]{3,0,1,2:T(8,128)}, f32[128,2,2,1024]{3,0,1,2:T(8,128)S(1)}, u32[]{:S(2)}) copy-start(f32[128,2,2,1024]{3,0,1,2:T(8,128)S(1)} %get-tuple-element.24) | copy-start | bytes 6291460
  37.7 24.9 %collective-permute-start.1 = (bf16[128,2,2,1024]{3,0,1,2:T(8,128)(2,1)S(1)}, bf16[128,2,2,1024]{3,0,1,2:T(8,128)(2,1)S(1)}, u32[]{:S(2)}, u32[]{:S(2)}) collective-permute-start(bf16[128,2,2,1024]{3,0,1,2:T(8,128)(2,1)S(1)} %get-tuple-element.25), channel_id=1, source_target_pairs={{0,4},{4,0},{8,12},{12,8},{16,20},{20,16},{24,28},{28,24},{32,36},... | collective-permute-start | bytes 3145736 | tf_op jit(solution)/shard_map/ppermute | solution.py:8
  62.8 1.4 copy-start.5
  65.2 111.0 %all-gather.5.cloned.1.call-start = ((), (), s32[]{:S(2)}) async-start(), calls=%async_computation | async-start | bytes 5242880 | tf_op jit(solution)/shard_map/all_gather | solution.py:60
  65.2 24.4 %collective-permute-start = (bf16[128,2,2,1024]{3,0,1,2:T(8,128)(2,1)}, bf16[128,2,2,1024]{3,0,1,2:T(8,128)(2,1)}, u32[]{:S(2)}, u32[]{:S(2)}) collective-permute-start(bf16[128,2,2,1024]{3,0,1,2:T(8,128)(2,1)} %get-tuple-element.26), channel_id=1, source_target_pairs={{0,4},{4,0},{8,12},{12,8},{16,20},{20,16},{24,28},{28,24},{32,36},... | collective-permute-start | bytes 3145736 | tf_op jit(solution)/shard_map/ppermute | solution.py:8
  69.7 206.3 %all-gather.11.cloned.1.call-start = ((), (), s32[]{:S(2)}) async-start(), calls=%async_computation.3 | async-start | bytes 2621440 | tf_op jit(solution)/shard_map/all_gather | solution.py:91
  133.5 1.6 copy-start
  176.1 2.8 copy-start.3
  180.5 1.2 copy-start.7
  180.5 1.5 copy-start.8
  183.5 1.4 copy-start.9
  183.5 55.9 %copy-start.6 = (f32[128,2,2,1024]{3,0,1,2:T(8,128)}, f32[128,2,2,1024]{3,0,1,2:T(8,128)S(1)}, u32[]{:S(2)}) copy-start(f32[128,2,2,1024]{3,0,1,2:T(8,128)S(1)} %get-tuple-element.12) | copy-start | bytes 6291460
  184.8 49.3 %collective-permute-start.2 = (f32[128,2,2,1024]{3,0,1,2:T(8,128)S(1)}, f32[128,2,2,1024]{3,0,1,2:T(8,128)S(1)}, u32[]{:S(2)}, u32[]{:S(2)}) collective-permute-start(f32[128,2,2,1024]{3,0,1,2:T(8,128)S(1)} %get-tuple-element.13), channel_id=1, source_target_pairs={{0,8},{4,12},{8,0},{12,4},{16,24},{20,28},{24,16},{28,20},{32,40},... | collective-permute-start | bytes 6291464 | tf_op jit(solution)/shard_map/ppermute | solution.py:8
  234.1 1.3 copy-start.11
  236.4 104.6 %all-gather.9.cloned.1.call-start = ((), (), s32[]{:S(2)}) async-start(), calls=%async_computation.2 | async-start | bytes 5242880 | tf_op jit(solution)/shard_map/all_gather | solution.py:60
  292.6 2.9 copy-start.10
  296.2 1.6 copy-start.1
  341.0 4.3 %copy-start.2 = (bf16[512,2,2,1024]{3,0,1,2:T(8,128)(2,1)S(1)}, bf16[512,2,2,1024]{3,0,1,2:T(8,128)(2,1)}, u32[]{:S(2)}) copy-start(bf16[512,2,2,1024]{3,0,1,2:T(8,128)(2,1)} %all-gather.9.cloned.1.call-done) | copy-start | bytes 12582916
  346.5 0.7 copy-start.13
Sparse Core Ops, SparseCore 0:
  65.3 46.1 all-gather.6
  113.3 62.8 all-gather.4
  236.6 39.3 all-gather.10
  278.2 62.8 all-gather.8
where the time goes:
time: 366 us; the launch traced here: 365 us
  waiting for transfers between devices  219 us (60%)
  local copies, waits for them, and re-layouts  66.7 us (18%)
  other arithmetic  29.4 us (8%)
  matrix products  20.1 us (5%)
  between operations  14.3 us (4%)
  blocking collectives  9.25 us (3%)
  starting transfers between devices  6.4 us (2%)
    ppermute x3, waiting for transfers between devices, swapped(): lax.ppermute(shard, axis, [(i, i ^ 1 << distance) for i in range(lax.axis...  89.4 us
    all_gather x2, waiting for transfers between devices, eliminate(): row_piece = lax.all_gather(coupling_rows, 'tile', axis=0, tiled=True)  77 us
    all_gather x2, waiting for transfers between devices, per_device(): interior = lax.all_gather(interior_rows, 'tile', axis=0, tiled=True)  52.2 us
    dot_general x32, matrix products, single(): jnp.einsum('mek,ken->men', first_part, second_part, preferred_element_typ...  20.1 us
    unnamed x30, local copies, waits for them, and re-layouts  18.5 us
    gather x2, local copies, waits for them, and re-layouts, per_device(): canonical = jnp.take(stored, column_source[0], axis=4)  18.3 us
    gather x2, local copies, waits for them, and re-layouts, inverse_guess(): diagonal = jnp.diagonal(values, axis1=0, axis2=3)  14.7 us
    transpose x2, local copies, waits for them, and re-layouts, inverse_guess(): diagonal = jnp.diagonal(values, axis1=0, axis2=3)  10.5 us
  transfers between devices with their start and end apart: 7, of which 7 were waited for; matrix products, arithmetic and copies ran while one was open for 17% of the time, Pallas kernels for 0%

commit v1 on v0

--- a/solution.py
+++ b/solution.py
@@ -57,7 +57,9 @@
     applied = complex_product(outer_coupling.astype(jnp.bfloat16), approx_inverse)
     middle = complex_product(applied.astype(jnp.bfloat16), interior).astype(jnp.bfloat16)
     reduced = (2.0 * applied - complex_product(middle, approx_inverse)).astype(jnp.bfloat16)
-    row_piece = lax.all_gather(coupling_rows, "tile", axis=0, tiled=True)
+    row_piece = jnp.concatenate(
+        lax.all_to_all(jnp.stack([coupling_rows] * lax.axis_size("tile")), "tile", 0, 0), axis=0
+    )
     columns = lax.slice_in_dim(reduced, 0, row_piece.shape[0], axis=3)
     return start_block - complex_product(columns, row_piece)
 

time: 366 us -> 414 us (1.13)
  waiting for transfers between devices: 219 us -> 245 us
  starting transfers between devices: 6.4 us -> 16.6 us
  blocking collectives: 9.25 us -> 18.7 us
  local copies, waits for them, and re-layouts: 66.7 us -> 75.6 us
  matrix products: 20.1 us -> 15.1 us
    all_to_all x0 -> x2, waiting for transfers between devices: none -> 99.6 us  [eliminate(): lax.all_to_all(jnp.stack([coupling_rows] * lax.axis_size('tile')), 'tile'...]
    all_gather x2 -> x0, waiting for transfers between devices: 77 us -> none  [eliminate(): row_piece = lax.all_gather(coupling_rows, 'tile', axis=0, tiled=True)]
    all_to_all x0 -> x2, starting transfers between devices: none -> 13.3 us  [eliminate(): lax.all_to_all(jnp.stack([coupling_rows] * lax.axis_size('tile')), 'tile'...]
    all_gather x2, waiting for transfers between devices: 52.2 us -> 63.4 us  [per_device(): interior = lax.all_gather(interior_rows, 'tile', axis=0, tiled=True)]
    psum x1, blocking collectives: 9.25 us -> 18.7 us  [per_device(): density = lax.psum(partial_sum, 'energy')]
    ppermute x3, waiting for transfers between devices: 89.4 us -> 81.6 us  [swapped(): lax.ppermute(shard, axis, [(i, i ^ 1 << distance) for i in range(lax.axis...]
    all_to_all x0 -> x2, local copies, waits for them, and re-layouts: none -> 5.26 us  [eliminate(): lax.all_to_all(jnp.stack([coupling_rows] * lax.axis_size('tile')), 'tile'...]
    another operation x1 -> x3, local copies, waits for them, and re-layouts: 0.9 us -> 6.13 us  [the longest x2 5.23 us: eliminate(): jnp.stack([coupling_rows] * lax.axis_size('tile'))]
  transfers between devices with their start and end apart: 7 -> 7, of which waited for: 7 -> 7; matrix products, arithmetic and copies ran while one was open for 17% -> 16% of each run, Pallas kernels for 0% -> 0%
where the time goes in v1:
time: 414 us; the launch traced here: 412 us
  waiting for transfers between devices  245 us (59%)
  local copies, waits for them, and re-layouts  75.6 us (18%)
  other arithmetic  27.3 us (7%)
  blocking collectives  18.7 us (5%)
  starting transfers between devices  16.6 us (4%)
  matrix products  15.1 us (4%)
  between operations  14.6 us (4%)
    all_to_all x2, waiting for transfers between devices, eliminate(): lax.all_to_all(jnp.stack([coupling_rows] * lax.axis_size('tile')), 'tile'...  99.6 us
    ppermute x3, waiting for transfers between devices, swapped(): lax.ppermute(shard, axis, [(i, i ^ 1 << distance) for i in range(lax.axis...  81.6 us
    all_gather x2, waiting for transfers between devices, per_device(): interior = lax.all_gather(interior_rows, 'tile', axis=0, tiled=True)  63.4 us
    psum x1, blocking collectives, per_device(): density = lax.psum(partial_sum, 'energy')  18.7 us
    gather x2, local copies, waits for them, and re-layouts, per_device(): canonical = jnp.take(stored, column_source[0], axis=4)  18.3 us
    unnamed x26, local copies, waits for them, and re-layouts  18.1 us
    dot_general x32, matrix products, single(): jnp.einsum('mek,ken->men', first_part, second_part, preferred_element_typ...  15.1 us
    gather x2, local copies, waits for them, and re-layouts, inverse_guess(): diagonal = jnp.diagonal(values, axis1=0, axis2=3)  13.6 us
  transfers between devices with their start and end apart: 7, of which 7 were waited for; matrix products, arithmetic and copies ran while one was open for 16% of the time, Pallas kernels for 0%

profile of v1, /device:TPU:2, one launch (start us, length us, event | category | flops | bytes accessed | tf_op | source)
XLA Modules:
  0.0 412.5 jit_solution(1801200762063886548)
XLA Ops:
  7.2 8.9 %copy.65 = bf16[1,2,128,2,2,1024]{2,4,5,3,1,0:T(2,128)(2,1)S(1)} copy(bf16[1,2,128,2,2,1024]{5,4,3,2,1,0:T(2,128)(2,1)} %param.3) | data formatting | bytes 4194304 | tf_op args[0]
  16.2 12.1 %gather_fusion = bf16[1024,2,128,2,2]{2,4,3,1,0:T(2,128)(2,1)} fusion(bf16[2,128,2,2,1024]{1,3,4,2,0:T(2,128)(2,1)S(1)} %bitcast.265, s32[1024]{0:T(1024)S(1)} %broadcast_clamp_fusion), kind=kCustom, calls=%fused_computation | custom fusion | bytes 4198400 | tf_op jit(solution)/shard_map/jit(_take)/gather | solution.py:69
  28.3 6.2 %copy.66 = bf16[1024,2,128,2,2]{0,2,3,4,1:T(8,128)(2,1)} copy(bf16[1024,2,128,2,2]{2,4,3,1,0:T(2,128)(2,1)} %gather_fusion) | data formatting | bytes 4194304 | tf_op jit(solution)/shard_map/jit(_take)/gather | solution.py:69
  34.5 1.8 select_bitcast_fusion
  36.3 1.4 fusion.58
  37.7 1.6 collective-permute-start.1
  39.3 23.3 %collective-permute-done.1 = bf16[128,2,2,1024]{3,0,1,2:T(8,128)(2,1)S(1)} collective-permute-done((bf16[128,2,2,1024]{3,0,1,2:T(8,128)(2,1)S(1)}, bf16[128,2,2,1024]{3,0,1,2:T(8,128)(2,1)S(1)}, u32[]{:S(2)}, u32[]{:S(2)}) %collective-permute-start.1) | collective-permute-done | bytes 1048608 | tf_op jit(solution)/shard_map/ppermute | solution.py:8
  62.8 1.3 copy-done.3
  64.2 0.9 fusion.36
  65.1 1.7 collective-permute-start
  66.8 1.7 select_convert_fusion.3
  68.6 2.6 stack.88
  71.2 8.5 %all-to-all-start = ((bf16[4,128,2,2,1024]{4,1,2,3,0:T(8,128)(2,1)}), bf16[4,128,2,2,1024]{4,1,2,3,0:T(8,128)(2,1)}, u32[]{:S(2)}, u32[]{:S(2)}) async-start(bf16[4,128,2,2,1024]{4,1,2,3,0:T(8,128)(2,1)} %stack.88), calls=%async_computation | async-start | bytes 8388608 | tf_op jit(solution)/shard_map/all_to_all | solution.py:61
  79.8 9.8 %collective-permute-done = bf16[128,2,2,1024]{3,0,1,2:T(8,128)(2,1)} collective-permute-done((bf16[128,2,2,1024]{3,0,1,2:T(8,128)(2,1)}, bf16[128,2,2,1024]{3,0,1,2:T(8,128)(2,1)}, u32[]{:S(2)}, u32[]{:S(2)}) %collective-permute-start) | collective-permute-done | bytes 1048608 | tf_op jit(solution)/shard_map/ppermute | solution.py:8
  89.6 1.8 convert_select_fusion.1
  91.5 1.1 slice.266
  92.6 1.0 slice.267
  93.7 24.8 %all-gather.3.cloned.1.call-done = bf16[512,2,2,512]{3,0,1,2:T(8,128)(2,1)} async-done(((bf16[128,2,2,512]{3,0,1,2:T(8,128)(2,1)}), bf16[512,2,2,512]{3,0,1,2:T(8,128)(2,1)}) %all-gather.3.cloned.1.call-update) | async-done | bytes 2097168 | tf_op jit(solution)/shard_map/all_gather | solution.py:93
  118.5 4.2 %fusion.65 = (f32[512,2,2,512]{3,0,1,2:T(8,128)}, f32[2,2,512,512]{3,2,0,1:T(8,128)S(1)}) fusion(bf16[512,2,2,512]{3,0,1,2:T(8,128)(2,1)} %all-gather.3.cloned.1.call-done), kind=kLoop, calls=%fused_computation.154 | loop fusion | flops 1048576 | bytes 10485760 | tf_op jit(solution)/shard_map/convert_element_type | solution.py:24
  122.7 5.2 %copy.68 = f32[2,2,512,512]{3,1,2,0:T(2,128)} copy(f32[2,2,512,512]{3,2,0,1:T(8,128)S(1)} %get-tuple-element.23) | data formatting | bytes 8388608 | tf_op jit(solution)/shard_map/jit(diagonal)/transpose | solution.py:25
  127.9 6.8 %gather_fusion.1 = f32[512,2,2]{0,2,1:T(2,128)S(1)} fusion(f32[2,2,512,512]{3,1,2,0:T(2,128)} %copy.68, s32[512]{0:T(512)S(1)} %bitcast.255), kind=kCustom, calls=%fused_computation.1 | custom fusion | bytes 20480 | tf_op jit(solution)/shard_map/jit(diagonal)/gather | solution.py:25
  134.7 2.9 fusion.31
  137.6 0.5 fusion.61
  138.1 0.5 fusion.14
  138.7 0.5 fusion.59
  139.2 0.5 fusion.13
  140.0 1.4 copy-done
  141.4 0.5 fusion.38
  141.9 0.5 fusion.18
  142.4 0.5 fusion.68
  143.0 0.5 fusion.39
  143.5 0.5 fusion.17
  144.1 0.5 fusion.12
  144.6 0.5 fusion.69
  145.1 0.5 fusion.11
  146.1 52.9 %all-to-all-done = bf16[4,128,2,2,1024]{4,1,2,3,0:T(8,128)(2,1)} async-done(((bf16[4,128,2,2,1024]{4,1,2,3,0:T(8,128)(2,1)}), bf16[4,128,2,2,1024]{4,1,2,3,0:T(8,128)(2,1)}, u32[]{:S(2)}, u32[]{:S(2)}) %all-to-all-start) | async-done | bytes 4194336 | tf_op jit(solution)/shard_map/all_to_all | solution.py:61
  199.0 2.6 copy.67
  201.6 0.8 fusion.3
  202.4 0.8 fusion.2
  203.2 0.8 subtract_bitcast_fusion
  204.0 0.8 add_bitcast_fusion
  205.5 0.7 fusion
  206.3 0.6 fusion.63
  206.9 1.3 copy-done.7
  208.2 48.5 %collective-permute-done.2 = f32[128,2,2,1024]{3,0,1,2:T(8,128)S(1)} collective-permute-done((f32[128,2,2,1024]{3,0,1,2:T(8,128)S(1)}, f32[128,2,2,1024]{3,0,1,2:T(8,128)S(1)}, u32[]{:S(2)}, u32[]{:S(2)}) %collective-permute-start.2) | collective-permute-done | bytes 2097184 | tf_op jit(solution)/shard_map/ppermute | solution.py:8
  256.7 1.3 copy-done.9
  258.0 1.0 fusion.35
  259.0 1.7 select_convert_fusion.1
  260.8 2.6 stack.98
  263.5 4.9 %all-to-all-start.1 = ((bf16[4,128,2,2,1024]{4,1,2,3,0:T(8,128)(2,1)}), bf16[4,128,2,2,1024]{4,1,2,3,0:T(8,128)(2,1)}, u32[]{:S(2)}, u32[]{:S(2)}) async-start(bf16[4,128,2,2,1024]{4,1,2,3,0:T(8,128)(2,1)} %stack.98), calls=%async_computation.1 | async-start | bytes 8388608 | tf_op jit(solution)/shard_map/all_to_all | solution.py:61
  268.4 0.9 dynamic-slice_convert_fusion
  269.3 1.1 constant_dynamic-slice_fusion
  270.4 38.6 %all-gather.5.cloned.1.call-done = bf16[512,2,2,512]{3,0,1,2:T(8,128)(2,1)} async-done(((bf16[128,2,2,512]{3,0,1,2:T(8,128)(2,1)}), bf16[512,2,2,512]{3,0,1,2:T(8,128)(2,1)}) %all-gather.5.cloned.1.call-update) | async-done | bytes 2097168 | tf_op jit(solution)/shard_map/all_gather | solution.py:93
  309.0 4.2 %fusion.64 = (f32[512,2,2,512]{3,0,1,2:T(8,128)}, f32[2,2,512,512]{3,2,0,1:T(8,128)S(1)}) fusion(bf16[512,2,2,512]{3,0,1,2:T(8,128)(2,1)} %all-gather.5.cloned.1.call-done), kind=kLoop, calls=%fused_computation.153 | loop fusion | flops 1048576 | bytes 10485760 | tf_op jit(solution)/shard_map/convert_element_type | solution.py:24
  313.2 5.2 %copy.97 = f32[2,2,512,512]{3,1,2,0:T(2,128)} copy(f32[2,2,512,512]{3,2,0,1:T(8,128)S(1)} %get-tuple-element.21) | data formatting | bytes 8388608 | tf_op jit(solution)/shard_map/jit(diagonal)/transpose | solution.py:25
  318.4 6.8 %gather_fusion.2 = f32[512,2,2]{0,2,1:T(2,128)S(1)} fusion(f32[2,2,512,512]{3,1,2,0:T(2,128)} %copy.97, s32[512]{0:T(512)S(1)} %bitcast.256), kind=kCustom, calls=%fused_computation.2 | custom fusion | bytes 20480 | tf_op jit(solution)/shard_map/jit(diagonal)/gather | solution.py:25
  325.3 2.9 fusion.33
  329.4 0.9 copy-done.1
  332.9 46.7 %all-to-all-done.1 = bf16[4,128,2,2,1024]{4,1,2,3,0:T(8,128)(2,1)} async-done(((bf16[4,128,2,2,1024]{4,1,2,3,0:T(8,128)(2,1)}), bf16[4,128,2,2,1024]{4,1,2,3,0:T(8,128)(2,1)}, u32[]{:S(2)}, u32[]{:S(2)}) %all-to-all-start.1) | async-done | bytes 4194336 | tf_op jit(solution)/shard_map/all_to_all | solution.py:61
  379.6 2.6 copy.96
  383.2 0.5 fusion.22
  383.7 0.5 fusion.20
  385.1 18.7 %psum.7 = f32[1,64]{1,0:T(1,128)} all-reduce(f32[1,64]{1,0:T(1,128)S(1)} %bitcast.274), channel_id=1, replica_groups=mesh['energy'=4,'cluster'=16,'tile'=4] {'energy'}, use_global_device_ids=true, to_apply=%region_2.3 | all-reduce | flops 64 | bytes 512 | tf_op jit(solution)/shard_map/psum | solution.py:122
  403.9 1.8 copy.101
  (62 shorter events, 7.9 us)
Async XLA Ops:
  7.2 9.0 %copy-start.10 = (s32[1,1024]{1,0:T(1,128)S(1)}, s32[1,1024]{1,0:T(1,128)}, u32[]{:S(2)}) copy-start(s32[1,1024]{1,0:T(1,128)} %param.4) | copy-start | bytes 12292
  7.2 111.3 %all-gather.3.cloned.1.call-start = ((), (), s32[]{:S(2)}) async-start(), calls=%async_computation.2 | async-start | bytes 2621440 | tf_op jit(solution)/shard_map/all_gather | solution.py:93
  37.7 25.2 %copy-start.2 = (f32[128,2,2,1024]{3,0,1,2:T(8,128)}, f32[128,2,2,1024]{3,0,1,2:T(8,128)S(1)}, u32[]{:S(2)}) copy-start(f32[128,2,2,1024]{3,0,1,2:T(8,128)S(1)} %get-tuple-element.24) | copy-start | bytes 6291460
  37.7 24.9 %collective-permute-start.1 = (bf16[128,2,2,1024]{3,0,1,2:T(8,128)(2,1)S(1)}, bf16[128,2,2,1024]{3,0,1,2:T(8,128)(2,1)S(1)}, u32[]{:S(2)}, u32[]{:S(2)}) collective-permute-start(bf16[128,2,2,1024]{3,0,1,2:T(8,128)(2,1)S(1)} %get-tuple-element.25), channel_id=1, source_target_pairs={{0,4},{4,0},{8,12},{12,8},{16,20},{20,16},{24,28},{28,24},{32,36},... | collective-permute-start | bytes 3145736 | tf_op jit(solution)/shard_map/ppermute | solution.py:8
  62.8 1.3 copy-start.3
  65.1 24.4 %collective-permute-start = (bf16[128,2,2,1024]{3,0,1,2:T(8,128)(2,1)}, bf16[128,2,2,1024]{3,0,1,2:T(8,128)(2,1)}, u32[]{:S(2)}, u32[]{:S(2)}) collective-permute-start(bf16[128,2,2,1024]{3,0,1,2:T(8,128)(2,1)} %get-tuple-element.26), channel_id=1, source_target_pairs={{0,4},{4,0},{8,12},{12,8},{16,20},{20,16},{24,28},{28,24},{32,36},... | collective-permute-start | bytes 3145736 | tf_op jit(solution)/shard_map/ppermute | solution.py:8
  71.2 127.8 %all-to-all-start = ((bf16[4,128,2,2,1024]{4,1,2,3,0:T(8,128)(2,1)}), bf16[4,128,2,2,1024]{4,1,2,3,0:T(8,128)(2,1)}, u32[]{:S(2)}, u32[]{:S(2)}) async-start(bf16[4,128,2,2,1024]{4,1,2,3,0:T(8,128)(2,1)} %stack.88), calls=%async_computation | async-start | bytes 8388608 | tf_op jit(solution)/shard_map/all_to_all | solution.py:61
  79.7 229.3 %all-gather.5.cloned.1.call-start = ((), (), s32[]{:S(2)}) async-start(), calls=%async_computation.3 | async-start | bytes 2621440 | tf_op jit(solution)/shard_map/all_gather | solution.py:93
  139.8 1.6 copy-start
  204.0 1.2 copy-start.5
  204.0 1.5 copy-start.6
  206.8 1.3 copy-start.7
  206.9 61.6 %copy-start.4 = (f32[128,2,2,1024]{3,0,1,2:T(8,128)}, f32[128,2,2,1024]{3,0,1,2:T(8,128)S(1)}, u32[]{:S(2)}) copy-start(f32[128,2,2,1024]{3,0,1,2:T(8,128)S(1)} %get-tuple-element.12) | copy-start | bytes 6291460
  208.2 48.5 %collective-permute-start.2 = (f32[128,2,2,1024]{3,0,1,2:T(8,128)S(1)}, f32[128,2,2,1024]{3,0,1,2:T(8,128)S(1)}, u32[]{:S(2)}, u32[]{:S(2)}) collective-permute-start(f32[128,2,2,1024]{3,0,1,2:T(8,128)S(1)} %get-tuple-element.13), channel_id=1, source_target_pairs={{0,8},{4,12},{8,0},{12,4},{16,24},{20,28},{24,16},{28,20},{32,40},... | collective-permute-start | bytes 6291464 | tf_op jit(solution)/shard_map/ppermute | solution.py:8
  256.7 1.3 copy-start.9
  263.5 116.1 %all-to-all-start.1 = ((bf16[4,128,2,2,1024]{4,1,2,3,0:T(8,128)(2,1)}), bf16[4,128,2,2,1024]{4,1,2,3,0:T(8,128)(2,1)}, u32[]{:S(2)}, u32[]{:S(2)}) async-start(bf16[4,128,2,2,1024]{4,1,2,3,0:T(8,128)(2,1)} %stack.98), calls=%async_computation.1 | async-start | bytes 8388608 | tf_op jit(solution)/shard_map/all_to_all | solution.py:61
  325.3 2.9 copy-start.8
  328.8 1.6 copy-start.1
  384.4 0.7 copy-start.11
Sparse Core Ops, SparseCore 0:
  65.3 53.1 all-gather.2
  259.1 49.8 all-gather.4
